TPU v7x, 256 devices: a whole 4x4x8 slice. The times are simulated.
256 devices in a mesh: leaf: 16 (over y, x), panel: 16 (over z, core).
Axes of the slice: x: 4, y: 4, z: 8, core: 2. Of those that a mesh axis runs over, the one named last changes fastest.
Arguments:
- right_sides: bfloat16 [3, 49152, 128], P(None, ('leaf', 'panel')), may hold values from -6 to 6
- inverse_low: bfloat16 [49152, 3072], P(('leaf', 'panel')), may hold values from -1 to 1, as said below
- inverse_mid: bfloat16 [49152, 6144], P(('leaf', 'panel')), may hold values from -1 to 1, as said below
- inverse_top: bfloat16 [49152, 12288], P(('leaf', 'panel')), may hold values from -1 to 1, as said below
- update_low: bfloat16 [49152, 3072], P(('leaf', 'panel')), may hold values from -0.109375 to 0.109375
- update_mid: bfloat16 [49152, 6144], P(('leaf', 'panel')), may hold values from -0.078125 to 0.078125
- slots_low: int32 [16, 3072], replicated, may hold values from 0 to 6143, as said below
- slots_mid: int32 [8, 6144], replicated, may hold values from 0 to 12287, as said below
Outputs:
- solutions: bfloat16 [3, 49152, 128], P(None, ('leaf', 'panel'))
Inputs may be any that keep to these rules, and one draw needn't show every extreme that they name: `inverse_low`: within each supernode's rows, the block is lower triangular with a unit diagonal. `inverse_mid`: within each supernode's rows, the block is lower triangular with a unit diagonal. `inverse_top`: within each supernode's rows, the block is lower triangular with a unit diagonal. `slots_low`: each row lists 3072 distinct rows of the parent supernode. `slots_mid`: each row lists 6144 distinct rows of the parent supernode.
All inputs are finite; a program needn't handle non-finite values.
Results may differ from a plain program's by a relative error of at most 0.015.
Values may be sent and summed in bfloat16 or wider, within the bound.
A program may use at most 128 MiB of HBM per device.

v0:
```python
import jax
import jax.numpy as jnp
from jax import lax
from jax.sharding import PartitionSpec as P


def from_partner(value, axis, distance):
    return lax.ppermute(value, axis, [(i, i ^ 1 << distance) for i in range(lax.axis_size(axis))])


def gather_group(local_rows, span_bits):
    leaf_at = lax.axis_index("leaf")
    gathered = lax.all_gather(local_rows, "panel", axis=0, tiled=True)
    for bit_at in range(span_bits):
        partner = from_partner(gathered, "leaf", bit_at)
        upper_on = leaf_at >> bit_at & 1 == 1
        gathered = jnp.where(
            upper_on,
            jnp.concatenate([partner, gathered], 0),
            jnp.concatenate([gathered, partner], 0),
        )
    return gathered


def sum_group(values, span_bits):
    leaf_at = lax.axis_index("leaf")
    panel_count = lax.axis_size("panel")
    groups = 2**span_bits
    share_rows = values.shape[0] // (groups * panel_count)
    arranged = values.reshape(groups, panel_count * share_rows, values.shape[1])
    for bit_at in reversed(range(span_bits)):
        half_rows = arranged.shape[0] // 2
        upper_on = leaf_at >> bit_at & 1 == 1
        lower_half = arranged[:half_rows]
        upper_half = arranged[half_rows:]
        kept_half = jnp.where(upper_on, upper_half, lower_half)
        sent_half = jnp.where(upper_on, lower_half, upper_half)
        arranged = kept_half + from_partner(sent_half.astype(jnp.bfloat16), "leaf", bit_at).astype(
            sent_half.dtype
        )
    return lax.psum_scatter(arranged[0], "panel", scatter_dimension=0, tiled=True)


def on_device(
    right_sides, inverse_low, inverse_mid, inverse_top, update_low, update_mid, slots_low, slots_mid
):
    inverses = (inverse_low, inverse_mid, inverse_top)
    updates = (update_low, update_mid)
    lists = (slots_low, slots_mid)
    height = len(inverses)
    leaf_at = lax.axis_index("leaf")
    slot_rows = []
    for height_at in range(height - 1):
        node_at = leaf_at >> height_at
        slot_rows.append(lax.dynamic_index_in_dim(lists[height_at], node_at, 0, keepdims=False))
    solved = []
    carried = None
    for height_at in range(height):
        if height_at == 0:
            local_rows = right_sides[0]
        else:
            local_rows = (right_sides[height_at].astype(jnp.float32) - carried).astype(jnp.bfloat16)
        gathered = gather_group(local_rows, height_at)
        inverse = inverses[height_at]
        solved_now = jnp.dot(inverse, gathered, preferred_element_type=jnp.float32).astype(
            jnp.bfloat16
        )
        solved.append(solved_now)
        if height_at + 1 < height:
            products = lax.dot_general(
                updates[height_at],
                solved_now,
                (((0,), (0,)), ((), ())),
                preferred_element_type=jnp.float32,
            )
            spread = jax.ops.segment_sum(
                products, slot_rows[height_at], num_segments=2 * inverse.shape[1]
            )
            carried = sum_group(spread, height_at + 1)
    results = [None] * height
    above = None
    for height_at in reversed(range(height)):
        inverse = inverses[height_at]
        if height_at + 1 < height:
            parent = gather_group(above, height_at + 1)
            picked = jnp.take(parent, slot_rows[height_at], axis=0)
            correction = jnp.dot(updates[height_at], picked, preferred_element_type=jnp.float32)
            target = (solved[height_at].astype(jnp.float32) - correction).astype(jnp.bfloat16)
        else:
            target = solved[height_at]
        partial_value = lax.dot_general(
            inverse, target, (((0,), (0,)), ((), ())), preferred_element_type=jnp.float32
        )
        above = sum_group(partial_value, height_at).astype(jnp.bfloat16)
        results[height_at] = above
    return jnp.stack(results)


def solution(mesh):
    return jax.shard_map(
        on_device,
        mesh=mesh,
        in_specs=(
            P(None, ("leaf", "panel"), None),
            P(("leaf", "panel"), None),
            P(("leaf", "panel"), None),
            P(("leaf", "panel"), None),
            P(("leaf", "panel"), None),
            P(("leaf", "panel"), None),
            P(),
            P(),
        ),
        out_specs=P(None, ("leaf", "panel"), None),
        check_vma=False,
    )
```

profile of v0, /device:TPU:7, one launch (start us, length us, event | category | flops | bytes accessed | tf_op | source)
XLA Modules:
  0.0 905.4 jit_solution(6385455675521610305)
XLA Ops:
  6.5 1.7 fusion.53
  8.2 22.6 %all-gather = bf16[1,3072,128]{2,1,0:T(8,128)(2,1)S(1)} all-gather(bf16[1,192,128]{2,1,0:T(8,128)(2,1)S(1)} %get-tuple-element.15), channel_id=2, replica_groups=mesh['leaf'=16,'panel'=16] {'panel'}, dimensions={1}, use_global_device_ids=true | all-gather | bytes 835584 | tf_op jit(solution)/shard_map/all_gather | solution.py:13
  30.8 1.7 convolution_convert_fusion
  33.2 1.6 convolution_bitcast_fusion.4
  34.7 3.0 copy.40
  37.8 1.5 compare_select_fusion.1
  39.3 19.0 %scatter_custom_fusion = f32[6144,128]{1,0:T(8,128)} fusion(s32[3072]{0:T(1024)S(1)} %bitcast.104, f32[3072,128]{1,0:T(8,128)} %copy.40, f32[]{:T(128)} %constant.46.clone.1), kind=kCustom, calls=%fused_computation.49 | custom fusion | flops 393216 | bytes 3146240 | tf_op jit(solution)/shard_map/scatter-add | solution.py:76
  58.3 3.7 fusion.52
  62.0 3.1 copy.67
  65.1 3.0 copy.68
  68.1 1.7 fusion.27
  70.5 18.4 %collective-permute-done = bf16[1,3072,128]{1,2,0:T(8,128)(2,1)S(1)} collective-permute-done((bf16[1,3072,128]{1,2,0:T(8,128)(2,1)S(1)}, bf16[1,3072,128]{1,2,0:T(8,128)(2,1)S(1)}, u32[]{:S(2)}, u32[]{:S(2)}) %collective-permute-start) | collective-permute-done | bytes 786464 | tf_op jit(solution)/shard_map/ppermute | solution.py:8
  88.9 1.4 fusion.16
  90.3 3.1 copy.56
  93.6 53.6 %reduce-scatter.16.cloned.1.call-done = f32[192,128]{1,0:T(8,128)} async-done(((f32[3072,128]{1,0:T(8,128)}), f32[192,128]{1,0:T(8,128)}) %reduce-scatter.16.cloned.1.call-update) | async-done | bytes 98320
  148.3 20.1 %all_gather.16 = bf16[3072,128]{1,0:T(8,128)(2,1)S(1)} all-gather(bf16[192,128]{1,0:T(8,128)(2,1)S(1)} %copy.43), channel_id=1, replica_groups=mesh['leaf'=16,'panel'=16] {'panel'}, dimensions={0}, use_global_device_ids=true | all-gather | bytes 835584 | tf_op jit(solution)/shard_map/all_gather | solution.py:13
  169.0 1.6 compare_select_fusion
  170.6 16.9 %collective-permute-done.1 = bf16[3072,128]{1,0:T(8,128)(2,1)} collective-permute-done((bf16[3072,128]{1,0:T(8,128)(2,1)S(1)}, bf16[3072,128]{1,0:T(8,128)(2,1)}, u32[]{:S(2)}, u32[]{:S(2)}) %collective-permute-start.1) | collective-permute-done | bytes 786464 | tf_op jit(solution)/shard_map/ppermute | solution.py:8
  187.5 3.0 fusion.25
  191.2 2.2 convolution_bitcast_fusion.2
  193.4 3.6 copy.45
  197.0 36.7 %scatter_custom_fusion.1 = f32[12288,128]{1,0:T(8,128)} fusion(s32[6144]{0:T(1024)S(1)} %bitcast.101, f32[6144,128]{1,0:T(8,128)} %copy.45, f32[]{:T(128)} %constant.46.clone.1), kind=kCustom, calls=%fused_computation.21 | custom fusion | flops 786432 | bytes 6291968 | tf_op jit(solution)/shard_map/scatter-add | solution.py:76
  233.7 5.9 fusion.51
  239.6 3.5 copy.71
  243.2 3.5 copy.70
  246.7 2.4 select_convert_fusion.1
  249.2 1.2 collective-permute-start.2
  251.4 34.3 %collective-permute-done.2 = bf16[2,3072,128]{1,2,0:T(8,128)(2,1)S(1)} collective-permute-done((bf16[2,3072,128]{1,2,0:T(8,128)(2,1)S(1)}, bf16[2,3072,128]{1,2,0:T(8,128)(2,1)S(1)}, u32[]{:S(2)}, u32[]{:S(2)}) %collective-permute-start.2) | collective-permute-done | bytes 1572896 | tf_op jit(solution)/shard_map/ppermute | solution.py:8
  287.0 16.6 %collective-permute-done.3 = bf16[1,3072,128]{1,2,0:T(8,128)(2,1)S(1)} collective-permute-done((bf16[1,3072,128]{1,2,0:T(8,128)(2,1)S(1)}, bf16[1,3072,128]{1,2,0:T(8,128)(2,1)S(1)}, u32[]{:S(2)}, u32[]{:S(2)}) %collective-permute-start.3) | collective-permute-done | bytes 786464 | tf_op jit(solution)/shard_map/ppermute | solution.py:8
  303.6 1.4 add_bitcast_fusion.1
  305.1 3.1 copy.58
  308.3 56.0 %reduce-scatter.18.cloned.1.call-done = f32[192,128]{1,0:T(8,128)} async-done(((f32[3072,128]{1,0:T(8,128)}), f32[192,128]{1,0:T(8,128)}) %reduce-scatter.18.cloned.1.call-update) | async-done | bytes 98320
  365.5 20.1 %all_gather.17 = bf16[3072,128]{1,0:T(8,128)(2,1)S(1)} all-gather(bf16[192,128]{1,0:T(8,128)(2,1)S(1)} %copy.50), channel_id=1, replica_groups=mesh['leaf'=16,'panel'=16] {'panel'}, dimensions={0}, use_global_device_ids=true | all-gather | bytes 835584 | tf_op jit(solution)/shard_map/all_gather | solution.py:13
  386.1 18.4 %collective-permute-done.4 = bf16[3072,128]{1,0:T(8,128)(2,1)S(1)} collective-permute-done((bf16[3072,128]{1,0:T(8,128)(2,1)S(1)}, bf16[3072,128]{1,0:T(8,128)(2,1)S(1)}, u32[]{:S(2)}, u32[]{:S(2)}) %collective-permute-start.4) | collective-permute-done | bytes 786464 | tf_op jit(solution)/shard_map/ppermute | solution.py:8
  406.1 1.2 collective-permute-start.5
  407.3 35.4 %collective-permute-done.5 = bf16[6144,128]{1,0:T(8,128)(2,1)} collective-permute-done((bf16[6144,128]{1,0:T(8,128)(2,1)S(1)}, bf16[6144,128]{1,0:T(8,128)(2,1)}, u32[]{:S(2)}, u32[]{:S(2)}) %collective-permute-start.5) | collective-permute-done | bytes 1572896 | tf_op jit(solution)/shard_map/ppermute | solution.py:8
  442.7 11.1 %convolution_bitcast_fusion = f32[12288,128]{0,1:T(8,128)} fusion(bf16[192,12288]{1,0:T(8,128)(2,1)} %param.11, bf16[6144,128]{1,0:T(8,128)(2,1)} %copy-done.8, bf16[6144,128]{1,0:T(8,128)(2,1)} %collective-permute-done.5, pred[]{:T(512)S(6)} %eq.5), kind=kOutput, calls=%fused_computation.4 | convolution fusion | flops 1222139904 | bytes 14155777 | tf_op jit(solution)/shard_map/dot_general | solution.py:91
  453.8 3.3 select_convert_fusion
  457.2 1.2 collective-permute-start.6
  458.8 34.0 %collective-permute-done.6 = bf16[2,3072,128]{1,2,0:T(8,128)(2,1)S(1)} collective-permute-done((bf16[2,3072,128]{1,2,0:T(8,128)(2,1)S(1)}, bf16[2,3072,128]{1,2,0:T(8,128)(2,1)S(1)}, u32[]{:S(2)}, u32[]{:S(2)}) %collective-permute-start.6) | collective-permute-done | bytes 1572896 | tf_op jit(solution)/shard_map/ppermute | solution.py:8
  494.0 15.7 %collective-permute-done.7 = bf16[1,3072,128]{1,2,0:T(8,128)(2,1)S(1)} collective-permute-done((bf16[1,3072,128]{1,2,0:T(8,128)(2,1)S(1)}, bf16[1,3072,128]{1,2,0:T(8,128)(2,1)S(1)}, u32[]{:S(2)}, u32[]{:S(2)}) %collective-permute-start.7) | collective-permute-done | bytes 786464 | tf_op jit(solution)/shard_map/ppermute | solution.py:8
  509.7 1.4 add_bitcast_fusion
  511.2 3.1 copy.60
  514.3 57.0 %reduce-scatter.20.cloned.1.call-done = f32[192,128]{1,0:T(8,128)} async-done(((f32[3072,128]{1,0:T(8,128)}), f32[192,128]{1,0:T(8,128)}) %reduce-scatter.20.cloned.1.call-update) | async-done | bytes 98320
  572.5 20.1 %all_gather.18 = bf16[3072,128]{1,0:T(8,128)(2,1)S(1)} all-gather(bf16[192,128]{1,0:T(8,128)(2,1)S(1)} %copy.53), channel_id=1, replica_groups=mesh['leaf'=16,'panel'=16] {'panel'}, dimensions={0}, use_global_device_ids=true | all-gather | bytes 835584 | tf_op jit(solution)/shard_map/all_gather | solution.py:13
  592.5 10.2 %collective-permute-start.8 = (bf16[3072,128]{1,0:T(8,128)(2,1)S(1)}, bf16[3072,128]{1,0:T(8,128)(2,1)S(1)}, u32[]{:S(2)}, u32[]{:S(2)}) collective-permute-start(bf16[3072,128]{1,0:T(8,128)(2,1)S(1)} %all_gather.18), channel_id=1, source_target_pairs={{0,16},{16,0},{32,48},{48,32},{64,80},{80,64},{96,112},{112,96},{1... | collective-permute-start | bytes 2359304 | tf_op jit(solution)/shard_map/ppermute | solution.py:8
  602.8 18.2 %collective-permute-done.8 = bf16[3072,128]{1,0:T(8,128)(2,1)S(1)} collective-permute-done((bf16[3072,128]{1,0:T(8,128)(2,1)S(1)}, bf16[3072,128]{1,0:T(8,128)(2,1)S(1)}, u32[]{:S(2)}, u32[]{:S(2)}) %collective-permute-start.8) | collective-permute-done | bytes 786464 | tf_op jit(solution)/shard_map/ppermute | solution.py:8
  621.4 1.4 collective-permute-start.9
  622.9 35.1 %collective-permute-done.9 = bf16[6144,128]{1,0:T(8,128)(2,1)S(1)} collective-permute-done((bf16[6144,128]{1,0:T(8,128)(2,1)S(1)}, bf16[6144,128]{1,0:T(8,128)(2,1)S(1)}, u32[]{:S(2)}, u32[]{:S(2)}) %collective-permute-start.9) | collective-permute-done | bytes 1572896 | tf_op jit(solution)/shard_map/ppermute | solution.py:8
  657.9 12.1 %maximum_select_fusion.2 = bf16[12288,128]{1,0:T(8,128)(2,1)} fusion(bf16[6144,128]{1,0:T(8,128)(2,1)S(1)} %maximum_select_fusion.6, bf16[6144,128]{1,0:T(8,128)(2,1)S(1)} %collective-permute-done.9, pred[]{:T(512)S(6)} %eq.5), kind=kLoop, calls=%fused_computation.18 | loop fusion | flops 14155776 | bytes 6291457 | tf_op jit(solution)/shard_map/jit(_where)/select_n | solution.py:17
  670.0 23.4 %gather_fusion = bf16[6144,128]{1,0:T(8,128)(2,1)} fusion(bf16[12288,128]{1,0:T(8,128)(2,1)} %maximum_select_fusion.2, s32[6144]{0:T(1024)S(1)} %broadcast_clamp_fusion), kind=kCustom, calls=%fused_computation | custom fusion | bytes 3170304 | tf_op jit(solution)/shard_map/jit(_take)/gather | solution.py:86
  693.4 5.6 convolution_bitcast_fusion.1
  699.0 2.0 fusion.28
  701.9 16.3 %collective-permute-done.10 = bf16[1,3072,128]{1,2,0:T(8,128)(2,1)S(1)} collective-permute-done((bf16[1,3072,128]{1,2,0:T(8,128)(2,1)S(1)}, bf16[1,3072,128]{1,2,0:T(8,128)(2,1)S(1)}, u32[]{:S(2)}, u32[]{:S(2)}) %collective-permute-start.10) | collective-permute-done | bytes 786464 | tf_op jit(solution)/shard_map/ppermute | solution.py:8
  718.3 3.3 fusion.15
  721.6 3.1 copy.62
  724.8 56.4 %reduce-scatter.22.cloned.1.call-done = f32[192,128]{1,0:T(8,128)} async-done(((f32[3072,128]{1,0:T(8,128)}), f32[192,128]{1,0:T(8,128)}) %reduce-scatter.22.cloned.1.call-update) | async-done | bytes 98320
  782.3 20.1 %all_gather.19 = bf16[3072,128]{1,0:T(8,128)(2,1)S(1)} all-gather(bf16[192,128]{1,0:T(8,128)(2,1)S(1)} %copy.54), channel_id=1, replica_groups=mesh['leaf'=16,'panel'=16] {'panel'}, dimensions={0}, use_global_device_ids=true | all-gather | bytes 835584 | tf_op jit(solution)/shard_map/all_gather | solution.py:13
  802.8 18.6 %collective-permute-done.11 = bf16[3072,128]{1,0:T(8,128)(2,1)S(1)} collective-permute-done((bf16[3072,128]{1,0:T(8,128)(2,1)S(1)}, bf16[3072,128]{1,0:T(8,128)(2,1)S(1)}, u32[]{:S(2)}, u32[]{:S(2)}) %collective-permute-start.11) | collective-permute-done | bytes 786464 | tf_op jit(solution)/shard_map/ppermute | solution.py:8
  821.4 1.6 maximum_select_fusion.7
  823.0 12.7 %gather_fusion.1 = bf16[3072,128]{1,0:T(8,128)(2,1)} fusion(bf16[6144,128]{1,0:T(8,128)(2,1)} %maximum_select_fusion.7, s32[3072]{0:T(1024)S(1)} %broadcast_clamp_fusion.1), kind=kCustom, calls=%fused_computation.1 | custom fusion | bytes 1585152 | tf_op jit(solution)/shard_map/jit(_take)/gather | solution.py:86
  835.6 3.8 convolution_bitcast_fusion.3
  839.5 3.1 copy.64
  842.5 54.3 %reduce-scatter.24.cloned.1.call-done = f32[192,128]{1,0:T(8,128)} async-done(((f32[3072,128]{1,0:T(8,128)}), f32[192,128]{1,0:T(8,128)}) %reduce-scatter.24.cloned.1.call-update) | async-done | bytes 98320
  (94 shorter events, 17.2 us)
Async XLA Ops:
  6.5 184.6 %copy-start = (bf16[192,6144]{1,0:T(8,128)(2,1)S(1)}, bf16[192,6144]{1,0:T(8,128)(2,1)}, u32[]{:S(2)}) copy-start(bf16[192,6144]{1,0:T(8,128)(2,1)} %param.13) | copy-start | bytes 7077892
  6.5 26.6 %copy-start.7 = (bf16[192,3072]{1,0:T(8,128)(2,1)S(1)}, bf16[192,3072]{1,0:T(8,128)(2,1)}, u32[]{:S(2)}) copy-start(bf16[192,3072]{1,0:T(8,128)(2,1)} %param.12) | copy-start | bytes 3538948
  6.5 140.6 %reduce-scatter.16.cloned.1.call-start = ((), (), s32[]{:S(2)}) async-start(), calls=%async_computation.5 | async-start | bytes 1671168
  32.6 0.6 copy-start.13
  39.3 22.7 %copy-start.22 = (s32[1,3072]{1,0:T(1,128)}, s32[1,3072]{1,0:T(1,128)S(1)}, u32[]{:S(2)}) copy-start(s32[1,3072]{1,0:T(1,128)S(1)} %get-tuple-element.6) | copy-start | bytes 36868
  68.1 20.8 %copy-start.4 = (f32[3072,128]{0,1:T(8,128)S(1)}, f32[3072,128]{0,1:T(8,128)}, u32[]{:S(2)}) copy-start(f32[3072,128]{0,1:T(8,128)} %copy.67) | copy-start | bytes 4718596
  68.1 20.8 %copy-start.5 = (f32[3072,128]{0,1:T(8,128)S(1)}, f32[3072,128]{0,1:T(8,128)}, u32[]{:S(2)}) copy-start(f32[3072,128]{0,1:T(8,128)} %copy.68) | copy-start | bytes 4718596
  69.8 19.1 %collective-permute-start = (bf16[1,3072,128]{1,2,0:T(8,128)(2,1)S(1)}, bf16[1,3072,128]{1,2,0:T(8,128)(2,1)S(1)}, u32[]{:S(2)}, u32[]{:S(2)}) collective-permute-start(bf16[1,3072,128]{1,2,0:T(8,128)(2,1)S(1)} %fusion.27), channel_id=1, source_target_pairs={{0,16},{16,0},{32,48},{48,32},{64,80},{80,64},{96,112},{112,96},{1... | collective-permute-start | bytes 2359304 | tf_op jit(solution)/shard_map/ppermute | solution.py:8
  90.3 3.1 copy-start.17
  93.4 271.0 %reduce-scatter.18.cloned.1.call-start = ((), (), s32[]{:S(2)}) async-start(), calls=%async_computation.6 | async-start | bytes 1671168
  168.4 19.1 %collective-permute-start.1 = (bf16[3072,128]{1,0:T(8,128)(2,1)S(1)}, bf16[3072,128]{1,0:T(8,128)(2,1)}, u32[]{:S(2)}, u32[]{:S(2)}) collective-permute-start(bf16[3072,128]{1,0:T(8,128)(2,1)S(1)} %all_gather.16), channel_id=1, source_target_pairs={{0,16},{16,0},{32,48},{48,32},{64,80},{80,64},{96,112},{112,96},{1... | collective-permute-start | bytes 2359304 | tf_op jit(solution)/shard_map/ppermute | solution.py:8
  170.6 26.5 %copy-start.19 = (s32[1,6144]{1,0:T(1,128)}, s32[1,6144]{1,0:T(1,128)S(1)}, u32[]{:S(2)}) copy-start(s32[1,6144]{1,0:T(1,128)S(1)} %get-tuple-element.8) | copy-start | bytes 73732
  190.5 0.6 copy-start.14
  246.7 3.7 copy-start.2
  249.0 2.0 copy-start.1
  249.2 36.6 %collective-permute-start.2 = (bf16[2,3072,128]{1,2,0:T(8,128)(2,1)S(1)}, bf16[2,3072,128]{1,2,0:T(8,128)(2,1)S(1)}, u32[]{:S(2)}, u32[]{:S(2)}) collective-permute-start(bf16[2,3072,128]{1,2,0:T(8,128)(2,1)S(1)} %bitcast.95), channel_id=1, source_target_pairs={{0,32},{16,48},{32,0},{48,16},{64,96},{80,112},{96,64},{112,80},{1... | collective-permute-start | bytes 4718600 | tf_op jit(solution)/shard_map/ppermute | solution.py:8
  286.4 17.3 %collective-permute-start.3 = (bf16[1,3072,128]{1,2,0:T(8,128)(2,1)S(1)}, bf16[1,3072,128]{1,2,0:T(8,128)(2,1)S(1)}, u32[]{:S(2)}, u32[]{:S(2)}) collective-permute-start(bf16[1,3072,128]{1,2,0:T(8,128)(2,1)S(1)} %select_convert_fusion.4), channel_id=1, source_target_pairs={{0,16},{16,0},{32,48},{48,32},{64,80},{80,64},{96,112},{112,96},{1... | collective-permute-start | bytes 2359304 | tf_op jit(solution)/shard_map/ppermute | solution.py:8
  305.1 3.1 copy-start.16
  308.1 263.2 %reduce-scatter.20.cloned.1.call-start = ((), (), s32[]{:S(2)}) async-start(), calls=%async_computation.7 | async-start | bytes 1671168
  385.6 19.0 %collective-permute-start.4 = (bf16[3072,128]{1,0:T(8,128)(2,1)S(1)}, bf16[3072,128]{1,0:T(8,128)(2,1)S(1)}, u32[]{:S(2)}, u32[]{:S(2)}) collective-permute-start(bf16[3072,128]{1,0:T(8,128)(2,1)S(1)} %all_gather.17), channel_id=1, source_target_pairs={{0,16},{16,0},{32,48},{48,32},{64,80},{80,64},{96,112},{112,96},{1... | collective-permute-start | bytes 2359304 | tf_op jit(solution)/shard_map/ppermute | solution.py:8
  405.0 1.2 copy-start.8
  406.1 36.5 %collective-permute-start.5 = (bf16[6144,128]{1,0:T(8,128)(2,1)S(1)}, bf16[6144,128]{1,0:T(8,128)(2,1)}, u32[]{:S(2)}, u32[]{:S(2)}) collective-permute-start(bf16[6144,128]{1,0:T(8,128)(2,1)S(1)} %maximum_select_fusion.5), channel_id=1, source_target_pairs={{0,32},{16,48},{32,0},{48,16},{64,96},{80,112},{96,64},{112,80},{1... | collective-permute-start | bytes 4718600 | tf_op jit(solution)/shard_map/ppermute | solution.py:8
  453.8 4.6 copy-start.3
  457.2 35.6 %collective-permute-start.6 = (bf16[2,3072,128]{1,2,0:T(8,128)(2,1)S(1)}, bf16[2,3072,128]{1,2,0:T(8,128)(2,1)S(1)}, u32[]{:S(2)}, u32[]{:S(2)}) collective-permute-start(bf16[2,3072,128]{1,2,0:T(8,128)(2,1)S(1)} %bitcast.96), channel_id=1, source_target_pairs={{0,32},{16,48},{32,0},{48,16},{64,96},{80,112},{96,64},{112,80},{1... | collective-permute-start | bytes 4718600 | tf_op jit(solution)/shard_map/ppermute | solution.py:8
  493.4 16.3 %collective-permute-start.7 = (bf16[1,3072,128]{1,2,0:T(8,128)(2,1)S(1)}, bf16[1,3072,128]{1,2,0:T(8,128)(2,1)S(1)}, u32[]{:S(2)}, u32[]{:S(2)}) collective-permute-start(bf16[1,3072,128]{1,2,0:T(8,128)(2,1)S(1)} %select_convert_fusion.3), channel_id=1, source_target_pairs={{0,16},{16,0},{32,48},{48,32},{64,80},{80,64},{96,112},{112,96},{1... | collective-permute-start | bytes 2359304 | tf_op jit(solution)/shard_map/ppermute | solution.py:8
  514.2 108.6 %copy-start.20 = (s32[1,6144]{1,0:T(1,128)S(1)}, s32[1,6144]{1,0:T(1,128)}, u32[]{:S(2)}) copy-start(s32[1,6144]{1,0:T(1,128)} %copy-done.19) | copy-start | bytes 73732
  514.3 108.6 %copy-start.18 = (s32[6144,1]{0,1:T(1,128)S(1)}, s32[6144,1]{0,1:T(1,128)}, u32[]{:S(2)}) copy-start(s32[6144,1]{0,1:T(1,128)} %get-tuple-element.7) | copy-start | bytes 73732
  514.3 266.9 %reduce-scatter.22.cloned.1.call-start = ((), (), s32[]{:S(2)}) async-start(), calls=%async_computation.8 | async-start | bytes 1671168
  572.3 97.7 %copy-start.9 = (bf16[192,128]{0,1:T(8,128)(2,1)}, bf16[192,128]{0,1:T(8,128)(2,1)S(1)}, u32[]{:S(2)}) copy-start(bf16[192,128]{0,1:T(8,128)(2,1)S(1)} %copy.61) | copy-start | bytes 147460
  592.5 28.4 %collective-permute-start.8 = (bf16[3072,128]{1,0:T(8,128)(2,1)S(1)}, bf16[3072,128]{1,0:T(8,128)(2,1)S(1)}, u32[]{:S(2)}, u32[]{:S(2)}) collective-permute-start(bf16[3072,128]{1,0:T(8,128)(2,1)S(1)} %all_gather.18), channel_id=1, source_target_pairs={{0,16},{16,0},{32,48},{48,32},{64,80},{80,64},{96,112},{112,96},{1... | collective-permute-start | bytes 2359304 | tf_op jit(solution)/shard_map/ppermute | solution.py:8
  621.4 36.5 %collective-permute-start.9 = (bf16[6144,128]{1,0:T(8,128)(2,1)S(1)}, bf16[6144,128]{1,0:T(8,128)(2,1)S(1)}, u32[]{:S(2)}, u32[]{:S(2)}) collective-permute-start(bf16[6144,128]{1,0:T(8,128)(2,1)S(1)} %maximum_select_fusion.6), channel_id=1, source_target_pairs={{0,32},{16,48},{32,0},{48,16},{64,96},{80,112},{96,64},{112,80},{1... | collective-permute-start | bytes 4718600 | tf_op jit(solution)/shard_map/ppermute | solution.py:8
  670.0 23.4 %copy-start.15 = (bf16[128,192]{0,1:T(8,128)(2,1)S(1)}, bf16[128,192]{0,1:T(8,128)(2,1)}, u32[]{:S(2)}) copy-start(bf16[128,192]{0,1:T(8,128)(2,1)} %copy-done.14) | copy-start | bytes 147460
  701.0 17.2 %collective-permute-start.10 = (bf16[1,3072,128]{1,2,0:T(8,128)(2,1)S(1)}, bf16[1,3072,128]{1,2,0:T(8,128)(2,1)S(1)}, u32[]{:S(2)}, u32[]{:S(2)}) collective-permute-start(bf16[1,3072,128]{1,2,0:T(8,128)(2,1)S(1)} %fusion.28), channel_id=1, source_target_pairs={{0,16},{16,0},{32,48},{48,32},{64,80},{80,64},{96,112},{112,96},{1... | collective-permute-start | bytes 2359304 | tf_op jit(solution)/shard_map/ppermute | solution.py:8
  721.6 81.2 %copy-start.23 = (s32[1,3072]{1,0:T(1,128)S(1)}, s32[1,3072]{1,0:T(1,128)}, u32[]{:S(2)}) copy-start(s32[1,3072]{1,0:T(1,128)} %copy-done.22) | copy-start | bytes 36868
  721.6 81.2 %copy-start.21 = (s32[3072,1]{0,1:T(1,128)S(1)}, s32[3072,1]{0,1:T(1,128)}, u32[]{:S(2)}) copy-start(s32[3072,1]{0,1:T(1,128)} %get-tuple-element.5) | copy-start | bytes 36868
  724.7 172.1 %reduce-scatter.24.cloned.1.call-start = ((), (), s32[]{:S(2)}) async-start(), calls=%async_computation.9 | async-start | bytes 1671168
  782.2 39.2 %copy-start.11 = (bf16[192,128]{0,1:T(8,128)(2,1)}, bf16[192,128]{0,1:T(8,128)(2,1)S(1)}, u32[]{:S(2)}) copy-start(bf16[192,128]{0,1:T(8,128)(2,1)S(1)} %copy.63) | copy-start | bytes 147460
  802.4 19.0 %collective-permute-start.11 = (bf16[3072,128]{1,0:T(8,128)(2,1)S(1)}, bf16[3072,128]{1,0:T(8,128)(2,1)S(1)}, u32[]{:S(2)}, u32[]{:S(2)}) collective-permute-start(bf16[3072,128]{1,0:T(8,128)(2,1)S(1)} %all_gather.19), channel_id=1, source_target_pairs={{0,16},{16,0},{32,48},{48,32},{64,80},{80,64},{96,112},{112,96},{1... | collective-permute-start | bytes 2359304 | tf_op jit(solution)/shard_map/ppermute | solution.py:8
  823.0 12.7 %copy-start.6 = (bf16[192,3072]{1,0:T(8,128)(2,1)S(1)}, bf16[192,3072]{1,0:T(8,128)(2,1)}, u32[]{:S(2)}) copy-start(bf16[192,3072]{1,0:T(8,128)(2,1)} %param.9) | copy-start | bytes 3538948
  839.5 58.4 %copy-start.10 = (bf16[192,128]{0,1:T(8,128)(2,1)S(1)}, bf16[192,128]{0,1:T(8,128)(2,1)}, u32[]{:S(2)}) copy-start(bf16[192,128]{0,1:T(8,128)(2,1)} %copy-done.9) | copy-start | bytes 147460
  839.5 58.4 %copy-start.12 = (bf16[192,128]{0,1:T(8,128)(2,1)S(1)}, bf16[192,128]{0,1:T(8,128)(2,1)}, u32[]{:S(2)}) copy-start(bf16[192,128]{0,1:T(8,128)(2,1)} %copy-done.11) | copy-start | bytes 147460
Sparse Core Ops, SparseCore 0:
  93.5 53.6 reduce-scatter.15
  308.3 56.0 reduce-scatter.17
  514.4 56.9 reduce-scatter.19
  724.9 56.2 reduce-scatter.21
  842.7 54.0 reduce-scatter.23
where the time goes:
time: 913 us; the launch traced here: 905 us
  waiting for transfers between devices  555 us (61%)
  blocking collectives  103 us (11%)
  other arithmetic  92.3 us (10%)
  local copies, waits for them, and re-layouts  92.1 us (10%)
  matrix products  29.1 us (3%)
  starting transfers between devices  19.8 us (2%)
  between operations  13.7 us (2%)
    ppermute x12, waiting for transfers between devices, from_partner(): lax.ppermute(value, axis, [(i, i ^ 1 << distance) for i in range(lax.axis...  278 us
    unnamed x10, waiting for transfers between devices  277 us
    all_gather x5, blocking collectives, gather_group(): gathered = lax.all_gather(local_rows, 'panel', axis=0, tiled=True)  103 us
    scatter-add x2, other arithmetic, on_device(): jax.ops.segment_sum(products, slot_rows[height_at], num_segments=2 * inve...  55.7 us
    unnamed x64, local copies, waits for them, and re-layouts  36.7 us
    gather x2, local copies, waits for them, and re-layouts, on_device(): picked = jnp.take(parent, slot_rows[height_at], axis=0)  36.1 us
    dot_general x3, matrix products, on_device(): lax.dot_general(inverse, target, (((0,), (0,)), ((), ())), preferred_elem...  20.5 us
    ppermute x12, starting transfers between devices, from_partner(): lax.ppermute(value, axis, [(i, i ^ 1 << distance) for i in range(lax.axis...  19.6 us
  transfers between devices with their start and end apart: 17, of which 17 were waited for; matrix products, arithmetic and copies ran while one was open for 0% of the time, Pallas kernels for 0%

commit v1 on v0

v1 whole, which is shorter than its diff:
```python
import functools

import jax
import jax.numpy as jnp
from jax import lax
from jax.experimental import pallas as pl
from jax.experimental.pallas import tpu as pltpu
from jax.sharding import PartitionSpec as P

BF = jnp.bfloat16
F32 = jnp.float32
ROWS = 192
HALF = 96
VEC = 128
RING = 8
CORES = 2
SLAB = ROWS * CORES
STEP = 2 * SLAB
PANELS = RING * CORES
GATHERS = (1, 1, 2, 2, 4, 2, 1)
REDUCES = (1, 2, 4, 2, 2, 1, 1)
DATA_SEMS = 400


class Sems:
    def __init__(self, send, recv):
        self.send, self.recv, self.at = send, recv, 0

    def take(self):
        at = self.at
        self.at += 1
        return self.send.at[at], self.recv.at[at]


def kernel(
    rs, il, im, it, ul, um, sl, sm, out,
    wl, wm, wt, vl, vm, pick0, pick1, part,
    ag0, ag1, ag2, ag3, ag4, ag5, ag6,
    dr0, dr1, dr2, dr3, dr4, dr5, dr6,
    rp0, rp1, rp2, rp3, rp4, rp5, rp6,
    xr0, xr1, xr2, xr3, xr4, xr5, xr6,
    dsend, rsend, xsend, esend, erecv, pair_rows, solved,
    wsem, send_sem, recv_sem,
):
    gathers = (ag0, ag1, ag2, ag3, ag4, ag5, ag6)
    core_in = (dr0, dr1, dr2, dr3, dr4, dr5, dr6)
    ring_in = (rp0, rp1, rp2, rp3, rp4, rp5, rp6)
    leaf_in = (xr0, xr1, xr2, xr3, xr4, xr5, xr6)
    leaf = lax.axis_index("leaf")
    panel = lax.axis_index("panel")
    z = panel // 2
    c = panel % 2
    x = leaf % 4
    base = leaf - x

    def zmod(v):
        return (v + 2 * RING) % RING

    up = (leaf, zmod(z + 1) * 2 + c)
    down = (leaf, zmod(z - 1) * 2 + c)
    core = (leaf, z * 2 + 1 - c)

    def flip(v, d):
        if d == 1:
            return v + 1 - 2 * (v % 2)
        if d == 2:
            return (v + 2) % 4
        return 3 - v

    def leaf_peer(d):
        return (base + flip(x, d), panel)

    sems = Sems(send_sem, recv_sem)

    def remote(src, dst, device):
        send, recv = sems.take()
        copy = pltpu.make_async_remote_copy(
            src_ref=src, dst_ref=dst, send_sem=send, recv_sem=recv,
            device_id=device, device_id_type=pl.DeviceIdType.MESH,
        )
        copy.start()
        return copy

    loads = []
    for at, (src, dst) in enumerate(((il, wl), (ul, vl), (im, wm), (um, vm), (it, wt))):
        copy = pltpu.make_async_copy(src, dst, wsem.at[at])
        copy.start()
        loads.append(copy)

    barrier = pltpu.get_barrier_semaphore()
    for device in (up, down, core, leaf_peer(1), leaf_peer(2), leaf_peer(3)):
        pl.semaphore_signal(barrier, inc=1, device_id=device, device_id_type=pl.DeviceIdType.MESH)
    pl.semaphore_wait(barrier, 6)

    gather_at = [0]
    reduce_at = [0]
    swap_at = [0]

    def all_gather(nx, value, beside=None):
        buf = gathers[gather_at[0]]
        gather_at[0] += 1
        xi = x % nx
        buf[xi, z, c] = value
        sends = []
        if nx > 1:
            mine = buf.at[xi, z, c]
            for d in range(1, nx):
                sends.append(remote(mine, mine, leaf_peer(d)))
            for copy in sends:
                copy.wait_recv()
        own = buf.at[:, z, c]
        plus = remote(own, own, up)
        minus = remote(own, own, down)
        cores = [remote(own, own, core)]
        sends += [plus, minus]
        if beside is not None:
            beside()
        for s in range(1, 4):
            lower = buf.at[:, zmod(z - s), c]
            upper = buf.at[:, zmod(z + s), c]
            plus.wait_recv()
            if s < 3:
                nplus = remote(lower, lower, up)
            else:
                half = buf.at[:, zmod(z - s), c, pl.ds(0, HALF)]
                nplus = remote(half, half, up)
            cores.append(remote(lower, lower, core))
            minus.wait_recv()
            if s < 3:
                nminus = remote(upper, upper, down)
            else:
                half = buf.at[:, zmod(z + s), c, pl.ds(HALF, HALF)]
                nminus = remote(half, half, down)
            cores.append(remote(upper, upper, core))
            plus, minus = nplus, nminus
            sends += [plus, minus]
        plus.wait_recv()
        minus.wait_recv()
        far = buf.at[:, zmod(z + 4), c]
        cores.append(remote(far, far, core))
        for copy in cores:
            copy.wait_recv()
        for copy in sends + cores:
            copy.wait_send()
        return buf

    def reduce_scatter(nx):
        at = reduce_at[0]
        reduce_at[0] += 1
        cin, rin, lin = core_in[at], ring_in[at], leaf_in[at]
        order = (4, 3, -3, 2, -2, 1, -1, 0)
        cores = {}
        for off in order:
            zz = zmod(z + off)
            for xi in range(nx):
                dsend[xi, zz] = part[xi * PANELS + 2 * zz + 1 - c].astype(BF)
            piece = dsend.at[pl.ds(0, nx), zz]
            cores[off] = remote(piece, cin.at[:, zz], core)

        def total(off):
            zz = zmod(z + off)
            cores[off].wait_recv()
            return [part[xi * PANELS + 2 * zz + c] + cin[xi, zz].astype(F32) for xi in range(nx)]

        def half_added(values, ref, low):
            done = []
            for xi in range(nx):
                if low:
                    done.append(jnp.concatenate(
                        [values[xi][:HALF] + ref[xi, :HALF].astype(F32), values[xi][HALF:]], 0))
                else:
                    done.append(jnp.concatenate(
                        [values[xi][:HALF], values[xi][HALF:] + ref[xi, HALF:].astype(F32)], 0))
            return done

        def put(slot, values):
            for xi in range(nx):
                rsend[slot, xi] = values[xi].astype(BF)

        sends = []
        put(0, total(4))
        lo, hi = pl.ds(0, HALF), pl.ds(HALF, HALF)
        g = pl.ds(0, nx)
        plus = remote(rsend.at[0, g, lo], rin.at[0, 0, :, lo], up)
        minus = remote(rsend.at[0, g, hi], rin.at[1, 0, :, hi], down)
        sends += [plus, minus]
        for s in range(1, 4):
            for sign in (0, 1):
                off = (4 - s) if sign == 0 else s - 4
                values = total(off)
                (plus, minus)[sign].wait_recv()
                got = rin.at[sign, s - 1]
                if s == 1:
                    values = half_added(values, got, sign == 0)
                else:
                    values = [values[xi] + got[xi].astype(F32) for xi in range(nx)]
                slot = 2 * s - 1 + sign
                put(slot, values)
                nxt = remote(rsend.at[slot, g], rin.at[sign, s], (up, down)[sign])
                sends.append(nxt)
                if sign == 0:
                    plus = nxt
                else:
                    minus = nxt
        values = total(0)
        plus.wait_recv()
        minus.wait_recv()
        values = [
            values[xi] + rin[0, 3, xi].astype(F32) + rin[1, 3, xi].astype(F32) for xi in range(nx)
        ]
        if nx == 1:
            result = values[0]
        else:
            for xi in range(nx):
                xsend[xi] = values[xi]
            moves = []
            for d in range(1, nx):
                esend[d] = xsend[flip(x, d) % nx].astype(BF)
                moves.append(remote(esend.at[d], lin.at[d], leaf_peer(d)))
            result = xsend[x % nx]
            for d in range(1, nx):
                moves[d - 1].wait_recv()
                result = result + lin[d].astype(F32)
            sends += moves
        for copy in sends + list(cores.values()):
            copy.wait_send()
        return result

    def swap(value, d):
        at = swap_at[0]
        swap_at[0] += 1
        esend[0] = value
        copy = remote(esend.at[0], erecv.at[at], leaf_peer(d))
        copy.wait_recv()
        got = erecv[at]
        copy.wait_send()
        return got

    def apply(weight, buf, nx, rows):
        def body(i, acc):
            lanes = pl.ds(pl.multiple_of(i * STEP, STEP), STEP)
            block = buf[i // 4, pl.ds((i % 4) * 2, 2)].reshape(STEP, VEC)
            return acc + jnp.dot(weight[:, lanes], block, preferred_element_type=F32)

        return lax.fori_loop(0, 4 * nx, body, jnp.zeros((rows, VEC), F32))

    def apply_t(weight, value, nx):
        def body(i, carry):
            lanes = pl.ds(pl.multiple_of(i * STEP, STEP), STEP)
            got = lax.dot_general(
                weight[:, lanes], value, (((0,), (0,)), ((), ())), preferred_element_type=F32
            )
            part[pl.ds(4 * i, 4)] = got.reshape(4, ROWS, VEC)
            return carry

        lax.fori_loop(0, 4 * nx, body, 0)

    def build_pick(pick, lists, row, nx, distance):
        here = (x % (2 * nx)) * (PANELS * ROWS) + panel * ROWS
        there = (flip(x, distance) % (2 * nx)) * (PANELS * ROWS) + panel * ROWS

        def body(i, carry):
            lanes = pl.ds(pl.multiple_of(i * SLAB, SLAB), SLAB)
            listed = lists[pl.ds(row, 1), lanes]
            at = lax.broadcasted_iota(jnp.int32, (ROWS, SLAB), 0)
            pick[pl.ds(0, ROWS), lanes] = jnp.where(at == listed - here, 1.0, 0.0).astype(BF)
            pick[pl.ds(ROWS, ROWS), lanes] = jnp.where(at == listed - there, 1.0, 0.0).astype(BF)
            return carry

        lax.fori_loop(0, 8 * nx, body, 0)

    def build_picks():
        build_pick(pick0, sl, leaf, 1, 1)
        build_pick(pick1, sm, leaf // 2, 2, 2)

    picks = (pick0, pick1)
    widths = (1, 2, 4)
    weights = (wl, wm, wt)
    updates = (vl, vm)
    load_of = {"w": (0, 2, 4), "v": (1, 3)}
    rhs = rs[0]
    for level in range(3):
        nx = widths[level]
        buf = all_gather(nx, rhs, build_picks if level == 0 else None)
        loads[load_of["w"][level]].wait()
        y = apply(weights[level], buf, nx, ROWS).astype(BF)
        solved[level] = y
        if level < 2:
            loads[load_of["v"][level]].wait()
            apply_t(updates[level], y, nx)
            mine = reduce_scatter(nx).astype(BF)
            buf = all_gather(nx, mine)
            chosen = apply(picks[level], buf, nx, SLAB)
            other = swap(chosen[ROWS:].astype(BF), nx)
            carried = chosen[:ROWS] + other.astype(F32)
            rhs = (rs[level + 1].astype(F32) - carried).astype(BF)
    target = solved[2]
    for level in (2, 1, 0):
        nx = widths[level]
        if level < 2:
            other = swap(above, nx)
            pair_rows[pl.ds(0, ROWS)] = above
            pair_rows[pl.ds(ROWS, ROWS)] = other
            apply_t(picks[level], pair_rows[...], nx)
            mine = reduce_scatter(nx).astype(BF)
            buf = all_gather(nx, mine)
            correction = apply(updates[level], buf, nx, ROWS)
            target = (solved[level].astype(F32) - correction).astype(BF)
        apply_t(weights[level], target, nx)
        above = reduce_scatter(nx).astype(BF)
        out[level] = above


def on_device(*args):
    vmem = pl.BlockSpec(memory_space=pltpu.VMEM)
    hbm = pl.BlockSpec(memory_space=pl.ANY)
    scratch = [
        pltpu.VMEM((ROWS, 3072), BF),
        pltpu.VMEM((ROWS, 6144), BF),
        pltpu.VMEM((ROWS, 12288), BF),
        pltpu.VMEM((ROWS, 3072), BF),
        pltpu.VMEM((ROWS, 6144), BF),
        pltpu.VMEM((SLAB, 3072), BF),
        pltpu.VMEM((SLAB, 6144), BF),
        pltpu.VMEM((4 * PANELS, ROWS, VEC), F32),
    ]
    scratch += [pltpu.VMEM((nx, RING, CORES, ROWS, VEC), BF) for nx in GATHERS]
    scratch += [pltpu.VMEM((nx, RING, ROWS, VEC), BF) for nx in REDUCES]
    scratch += [pltpu.VMEM((2, 4, nx, ROWS, VEC), BF) for nx in REDUCES]
    scratch += [pltpu.VMEM((nx, ROWS, VEC), BF) for nx in REDUCES]
    scratch += [
        pltpu.VMEM((4, RING, ROWS, VEC), BF),
        pltpu.VMEM((7, 4, ROWS, VEC), BF),
        pltpu.VMEM((4, ROWS, VEC), F32),
        pltpu.VMEM((4, ROWS, VEC), BF),
        pltpu.VMEM((4, ROWS, VEC), BF),
        pltpu.VMEM((SLAB, VEC), BF),
        pltpu.VMEM((3, ROWS, VEC), BF),
        pltpu.SemaphoreType.DMA((5,)),
        pltpu.SemaphoreType.DMA((DATA_SEMS,)),
        pltpu.SemaphoreType.DMA((DATA_SEMS,)),
    ]
    return pl.pallas_call(
        kernel,
        out_shape=jax.ShapeDtypeStruct((3, ROWS, VEC), BF),
        in_specs=[vmem, hbm, hbm, hbm, hbm, hbm, vmem, vmem],
        out_specs=vmem,
        scratch_shapes=scratch,
        compiler_params=pltpu.CompilerParams(
            collective_id=0, has_side_effects=True, vmem_limit_bytes=60 * 1024 * 1024
        ),
    )(*args)


def solution(mesh):
    split = P(("leaf", "panel"), None)
    return jax.shard_map(
        on_device,
        mesh=mesh,
        in_specs=(
            P(None, ("leaf", "panel"), None), split, split, split, split, split, P(), P(),
        ),
        out_specs=P(None, ("leaf", "panel"), None),
        check_vma=False,
    )
```

time: 913 us -> 326 us (0.36)
  waiting for transfers between devices: 555 us -> 0 us
  Pallas kernels: 0 us -> 320 us
  blocking collectives: 103 us -> 0 us
  other arithmetic: 92.3 us -> 0 us
  local copies, waits for them, and re-layouts: 92.1 us -> 1.58 us
  matrix products: 29.1 us -> 0 us
  starting transfers between devices: 19.8 us -> 0 us
  between operations: 13.7 us -> 0.01 us
    pallas_call x0 -> x1, Pallas kernels: none -> 320 us  [on_device(): pl.pallas_call(kernel, out_shape=jax.ShapeDtypeStruct((3, ROWS, VEC), BF)...]
    ppermute x12 -> x0, waiting for transfers between devices: 278 us -> none  [from_partner(): lax.ppermute(value, axis, [(i, i ^ 1 << distance) for i in range(lax.axis...]
    unnamed x10 -> x0, waiting for transfers between devices: 277 us -> none
    all_gather x5 -> x0, blocking collectives: 103 us -> none  [gather_group(): gathered = lax.all_gather(local_rows, 'panel', axis=0, tiled=True)]
    scatter-add x2 -> x0, other arithmetic: 55.7 us -> none  [on_device(): jax.ops.segment_sum(products, slot_rows[height_at], num_segments=2 * inve...]
    gather x2 -> x0, local copies, waits for them, and re-layouts: 36.1 us -> none  [on_device(): picked = jnp.take(parent, slot_rows[height_at], axis=0)]
    unnamed x64 -> x1, local copies, waits for them, and re-layouts: 36.7 us -> 1.58 us
    dot_general x7 -> x0, matrix products: 29.1 us -> none  [the longest x3 20.5 us: on_device(): lax.dot_general(inverse, target, (((0,), (0,)), ((), ())), preferred_elem...]
  transfers between devices with their start and end apart: 17 -> 0, of which waited for: 17 -> 0; matrix products, arithmetic and copies ran while one was open for 0% -> 0% of each run, Pallas kernels for 0% -> 0%
where the time goes in v1:
time: 326 us; the launch traced here: 322 us
  Pallas kernels  320 us (98%)
    pallas_call x1, Pallas kernels, on_device(): pl.pallas_call(kernel, out_shape=jax.ShapeDtypeStruct((3, ROWS, VEC), BF)...  320 us

profile of v1, /device:TPU:7, one launch (start us, length us, event | category | flops | bytes accessed | tf_op | source)
XLA Modules:
  0.0 321.6 jit_solution(13523807083036311661)
XLA Ops:
  0.0 320.0 %shard_map.82 = bf16[3,192,128]{2,1,0:T(8,128)(2,1)} custom-call(bf16[3,192,128]{2,1,0:T(8,128)(2,1)} %rs.1, bf16[192,3072]{1,0:T(8,128)(2,1)} %il.1, bf16[192,6144]{1,0:T(8,128)(2,1)} %im.1, bf16[192,12288]{1,0:T(8,128)(2,1)} %it.1, bf16[192,3072]{1,0:T(8,128)(2,1)} %ul.1, bf16[192,6144]{1,0:T(8,128)(2,1)} %um.1, s32[16,3072]{1,0:T(8,128)} %sl.1, s32[8,6144]{1,0:T(8,128)} %sm.1), custom_call_target="tpu_custom_call" | custom-call | tf_op jit(solution)/shard_map/pallas_call | solution.py:343
  320.0 1.6 copy.10

commit v2 on v0

v2 whole, which is shorter than its diff:
```python
import jax
import jax.numpy as jnp
from jax import lax
from jax.experimental import pallas as pl
from jax.experimental.pallas import tpu as pltpu
from jax.sharding import PartitionSpec as P

BF = jnp.bfloat16
F32 = jnp.float32
ROWS = 192
VEC = 128
RING = 8
CORES = 2
SLAB = ROWS * CORES
COLS = RING * SLAB
PHASES = 7
EXCHANGES = 8
PER_PHASE = 15
BULK_AT = 2 * PHASES * PER_PHASE + EXCHANGES * 3
DATA_SEMS = BULK_AT + 8
MESH = pl.DeviceIdType.MESH


def kernel(
    rs, il, im, it, ul, um, sl, sm, out,
    w0, w1, w2, v0, v1, pick0, pick1, part, acc, gathers, core_in, ring_in, leaf_in,
    dsend, rsend, esend, vals, solved, wsem, send_sem, recv_sem,
):
    leaf = lax.axis_index("leaf")
    panel = lax.axis_index("panel")
    z = panel // 2
    c = panel % 2
    x = leaf % 4
    xi = leaf % 2
    base = leaf - x

    def ring(off):
        return (z + off + RING) % RING

    def chip(off):
        return (leaf, ring(off) * 2 + c)

    core = (leaf, z * 2 + 1 - c)

    def flip(d):
        if d == 1:
            return x + 1 - 2 * xi
        if d == 2:
            return (x + 2) % 4
        return 3 - x

    def peer(d):
        return (base + flip(d), panel)

    def far_first(k):
        return jnp.where(k % 2 == 1, 4 + (k + 1) // 2, 4 - k // 2)

    def remote(at, src, dst, device):
        return pltpu.make_async_remote_copy(
            src_ref=src, dst_ref=dst, send_sem=send_sem.at[at], recv_sem=recv_sem.at[at],
            device_id=device, device_id_type=MESH,
        )

    def columns(block):
        return pl.ds(pl.multiple_of(block * COLS, COLS), COLS)

    def lanes(zz):
        return pl.ds(pl.multiple_of(zz * SLAB, SLAB), SLAB)

    mine = [
        pltpu.make_async_copy(il, w0.at[0], wsem.at[0]),
        pltpu.make_async_copy(ul, v0.at[0], wsem.at[1]),
        pltpu.make_async_copy(im.at[:, columns(xi)], w1.at[xi], wsem.at[2]),
        pltpu.make_async_copy(um.at[:, columns(xi)], v1.at[xi], wsem.at[3]),
        pltpu.make_async_copy(it.at[:, columns(x)], w2.at[x], wsem.at[4]),
    ]
    for copy in mine:
        copy.start()

    peers = [chip(off) for off in range(1, RING)] + [core] + [peer(d) for d in (1, 2, 3)]
    barrier = pltpu.get_barrier_semaphore()
    for device in peers:
        pl.semaphore_signal(barrier, inc=1, device_id=device, device_id_type=MESH)
    pl.semaphore_wait(barrier, len(peers))

    bulk_w1 = [remote(BULK_AT, im.at[:, columns(1 - xi)], w1.at[xi], peer(1))]
    bulk_v1 = [remote(BULK_AT + 1, um.at[:, columns(1 - xi)], v1.at[xi], peer(1))]
    bulk_w2 = [
        remote(BULK_AT + 1 + d, it.at[:, columns(flip(d))], w2.at[x], peer(d)) for d in (1, 2, 3)
    ]

    def start(copies):
        for copy in copies:
            copy.start()

    def arrive(copies):
        for copy in copies:
            copy.wait_recv()

    counts = {"gather": 0, "reduce": 0, "exchange": 0}

    def gather_apply(value, weight, nx, beside=None):
        at = counts["gather"]
        counts["gather"] += 1
        sem = at * PER_PHASE
        buf = gathers.at[at]
        gathers[at, z, c] = value

        def across(k):
            own = buf.at[z, c]
            return remote(sem + k, own, own, chip(far_first(k)))

        def source(kk):
            return ring(-far_first(7 - kk))

        def to_core(kk):
            block = buf.at[source(kk), c]
            return remote(sem + 7 + kk, block, block, core)

        to_core(0).start()

        def send(k, carry):
            across(k).start()
            return carry

        lax.fori_loop(0, 7, send, 0)
        acc[pl.ds(0, nx)] = jnp.zeros((nx, ROWS, VEC), F32)
        if beside is not None:
            beside()

        def use(kk):
            to_core(kk).wait_recv()
            zz = source(kk)
            slab = gathers[at, zz].reshape(SLAB, VEC)
            matrix = weight[:, :, lanes(zz)].reshape(nx * ROWS, SLAB)
            got = jnp.dot(matrix, slab, preferred_element_type=F32)
            acc[pl.ds(0, nx)] += got.reshape(nx, ROWS, VEC)

        def step(kk, carry):
            across(7 - kk).wait_recv()
            to_core(kk).start()
            use(kk - 1)
            return carry

        lax.fori_loop(1, 8, step, 0)
        use(7)

        def drain(k, carry):
            across(k).wait_send()
            to_core(k).wait_send()
            return carry

        lax.fori_loop(0, 7, drain, 0)
        to_core(7).wait_send()

    def apply_reduce(weight, nx):
        at = counts["reduce"]
        counts["reduce"] += 1
        sem = (PHASES + at) * PER_PHASE

        def to_core(k):
            return remote(sem + k, dsend.at[k], core_in.at[at, k], core)

        def across(k):
            return remote(sem + 8 + k, rsend.at[k], ring_in.at[at, k], chip(far_first(k)))

        def make(k):
            zz = ring(far_first(k))
            matrix = weight[:, :, lanes(zz)].reshape(nx * ROWS, SLAB)
            right = vals[pl.ds(0, nx)].reshape(nx * ROWS, VEC)
            got = lax.dot_general(
                matrix, right, (((0,), (0,)), ((), ())), preferred_element_type=F32
            )
            part[k] = got.reshape(CORES, ROWS, VEC)
            dsend[k] = part[k, 1 - c].astype(BF)
            to_core(k).start()

        def total(k):
            to_core(k).wait_recv()
            return part[k, c] + core_in[at, k].astype(F32)

        def send(k):
            rsend[k] = total(k).astype(BF)
            across(k).start()

        def first(k, carry):
            make(k)
            return carry

        def step(k, carry):
            make(k)
            send(k - 2)
            return carry

        lax.fori_loop(0, 2, first, 0)
        lax.fori_loop(2, 8, step, 0)
        send(6)

        def collect(i, value):
            k = 6 - i
            across(k).wait_recv()
            return value + ring_in[at, k].astype(F32)

        value = lax.fori_loop(0, 7, collect, total(7))

        def drain(k, carry):
            across(k).wait_send()
            to_core(k).wait_send()
            return carry

        lax.fori_loop(0, 7, drain, 0)
        to_core(7).wait_send()
        return value

    def exchange(distances, fill, width=1):
        at = counts["exchange"]
        counts["exchange"] += 1
        copies = {}
        for d in distances:
            fill(d)
            group = pl.ds(d, width)
            copies[d] = remote(
                2 * PHASES * PER_PHASE + at * 3 + d - 1, esend.at[group], leaf_in.at[at, group],
                peer(d),
            )
            copies[d].start()
        for d in distances:
            copies[d].wait_recv()
        for d in distances:
            copies[d].wait_send()
        return at

    def build_pick(pick, lists, row, first, nx):
        def body(i, carry):
            at = pl.multiple_of(i * SLAB, SLAB)
            listed = lists[pl.ds(row, 1), pl.ds(pl.multiple_of(first * COLS + at, SLAB), SLAB)]
            iota = lax.broadcasted_iota(jnp.int32, (ROWS, SLAB), 0)
            for owner in range(nx):
                hit = iota == listed - (owner * COLS + panel * ROWS)
                pick[owner, :, pl.ds(at, SLAB)] = jnp.where(hit, 1.0, 0.0).astype(BF)
            return carry

        lax.fori_loop(0, RING, body, 0)

    both = (0, 1)
    every = (1, 2, 3)

    def send_acc(d):
        esend[d] = acc[flip(d)].astype(BF)

    def send_acc_pair(d):
        for i in both:
            esend[1 + i] = acc[i].astype(BF)

    start(bulk_w1)
    mine[0].wait()
    gather_apply(rs[0], w0, 1, lambda: build_pick(pick0, sl, leaf, 0, 2))
    solved[0] = acc[0].astype(BF)
    vals[0] = solved[0]
    start(bulk_v1)
    mine[1].wait()
    summed = apply_reduce(v0, 1).astype(BF)
    gather_apply(summed, pick0, 2, lambda: build_pick(pick1, sm, leaf // 2, xi, 4))

    def send_other(d):
        esend[d] = acc[1 - xi].astype(BF)

    at = exchange((1,), send_other)
    carried = acc[xi] + leaf_in[at, 1].astype(F32)
    start(bulk_w2)

    mine[2].wait()
    arrive(bulk_w1)
    gather_apply((rs[1].astype(F32) - carried).astype(BF), w1, 2)
    at = exchange((1,), send_acc_pair, 2)
    for i in both:
        solved[1 + i] = (acc[i] + leaf_in[at, 1 + i].astype(F32)).astype(BF)
        vals[i] = solved[1 + i]
    mine[3].wait()
    arrive(bulk_v1)
    summed = apply_reduce(v1, 2).astype(BF)
    gather_apply(summed, pick1, 4)
    at = exchange(every, send_acc)
    carried = acc[x]
    for d in every:
        carried = carried + leaf_in[at, d].astype(F32)

    mine[4].wait()
    arrive(bulk_w2)
    gather_apply((rs[2].astype(F32) - carried).astype(BF), w2, 4)
    at = exchange(every, send_acc)
    top = acc[x]
    for d in every:
        top = top + leaf_in[at, d].astype(F32)

    def share(value, distances):
        def fill(d):
            esend[d] = value

        at = exchange(distances, fill)
        if len(distances) == 1:
            vals[xi] = value
            vals[1 - xi] = leaf_in[at, 1]
        else:
            vals[x] = value
            for d in distances:
                vals[flip(d)] = leaf_in[at, d]

    share(top.astype(BF), every)
    above = apply_reduce(w2, 4).astype(BF)
    out[2] = above

    share(above, every)
    summed = apply_reduce(pick1, 4).astype(BF)
    gather_apply(summed, v1, 2)
    at = exchange((1,), send_acc_pair, 2)
    for i in both:
        correction = acc[i] + leaf_in[at, 1 + i].astype(F32)
        vals[i] = (solved[1 + i].astype(F32) - correction).astype(BF)
    above = apply_reduce(w1, 2).astype(BF)
    out[1] = above

    share(above, (1,))
    summed = apply_reduce(pick0, 2).astype(BF)
    gather_apply(summed, v0, 1)
    vals[0] = (solved[0].astype(F32) - acc[0]).astype(BF)
    out[0] = apply_reduce(w0, 1).astype(BF)

    for copy in bulk_w1 + bulk_v1 + bulk_w2:
        copy.wait_send()


def on_device(*args):
    vmem = pl.BlockSpec(memory_space=pltpu.VMEM)
    hbm = pl.BlockSpec(memory_space=pl.ANY)
    scratch = [pltpu.VMEM((nx, ROWS, COLS), BF) for nx in (1, 2, 4, 1, 2, 2, 4)]
    scratch += [
        pltpu.VMEM((RING, CORES, ROWS, VEC), F32),
        pltpu.VMEM((4, ROWS, VEC), F32),
        pltpu.VMEM((PHASES, RING, CORES, ROWS, VEC), BF),
        pltpu.VMEM((PHASES, RING, ROWS, VEC), BF),
        pltpu.VMEM((PHASES, RING, ROWS, VEC), BF),
        pltpu.VMEM((EXCHANGES, 4, ROWS, VEC), BF),
        pltpu.VMEM((RING, ROWS, VEC), BF),
        pltpu.VMEM((RING, ROWS, VEC), BF),
        pltpu.VMEM((4, ROWS, VEC), BF),
        pltpu.VMEM((4, ROWS, VEC), BF),
        pltpu.VMEM((3, ROWS, VEC), BF),
        pltpu.SemaphoreType.DMA((5,)),
        pltpu.SemaphoreType.DMA((DATA_SEMS,)),
        pltpu.SemaphoreType.DMA((DATA_SEMS,)),
    ]
    return pl.pallas_call(
        kernel,
        out_shape=jax.ShapeDtypeStruct((3, ROWS, VEC), BF),
        in_specs=[vmem, hbm, hbm, hbm, hbm, hbm, vmem, vmem],
        out_specs=vmem,
        scratch_shapes=scratch,
        compiler_params=pltpu.CompilerParams(
            collective_id=0, has_side_effects=True, vmem_limit_bytes=56 * 1024 * 1024
        ),
    )(*args)


def solution(mesh):
    split = P(("leaf", "panel"), None)
    return jax.shard_map(
        on_device,
        mesh=mesh,
        in_specs=(
            P(None, ("leaf", "panel"), None), split, split, split, split, split, P(), P(),
        ),
        out_specs=P(None, ("leaf", "panel"), None),
        check_vma=False,
    )
```

time: 913 us -> 287 us (0.31)
  waiting for transfers between devices: 555 us -> 0 us
  Pallas kernels: 0 us -> 284 us
  blocking collectives: 103 us -> 0 us
  other arithmetic: 92.3 us -> 0 us
  local copies, waits for them, and re-layouts: 92.1 us -> 1.58 us
  matrix products: 29.1 us -> 0 us
  starting transfers between devices: 19.8 us -> 0 us
  between operations: 13.7 us -> 0.01 us
    pallas_call x0 -> x1, Pallas kernels: none -> 284 us  [on_device(): pl.pallas_call(kernel, out_shape=jax.ShapeDtypeStruct((3, ROWS, VEC), BF)...]
    ppermute x12 -> x0, waiting for transfers between devices: 278 us -> none  [from_partner(): lax.ppermute(value, axis, [(i, i ^ 1 << distance) for i in range(lax.axis...]
    unnamed x10 -> x0, waiting for transfers between devices: 277 us -> none
    all_gather x5 -> x0, blocking collectives: 103 us -> none  [gather_group(): gathered = lax.all_gather(local_rows, 'panel', axis=0, tiled=True)]
    scatter-add x2 -> x0, other arithmetic: 55.7 us -> none  [on_device(): jax.ops.segment_sum(products, slot_rows[height_at], num_segments=2 * inve...]
    gather x2 -> x0, local copies, waits for them, and re-layouts: 36.1 us -> none  [on_device(): picked = jnp.take(parent, slot_rows[height_at], axis=0)]
    unnamed x64 -> x1, local copies, waits for them, and re-layouts: 36.7 us -> 1.58 us
    dot_general x7 -> x0, matrix products: 29.1 us -> none  [the longest x3 20.5 us: on_device(): lax.dot_general(inverse, target, (((0,), (0,)), ((), ())), preferred_elem...]
  transfers between devices with their start and end apart: 17 -> 0, of which waited for: 17 -> 0; matrix products, arithmetic and copies ran while one was open for 0% -> 0% of each run, Pallas kernels for 0% -> 0%
where the time goes in v2:
time: 287 us; the launch traced here: 286 us
  Pallas kernels  284 us (99%)
    pallas_call x1, Pallas kernels, on_device(): pl.pallas_call(kernel, out_shape=jax.ShapeDtypeStruct((3, ROWS, VEC), BF)...  284 us

profile of v2, /device:TPU:7, one launch (start us, length us, event | category | flops | bytes accessed | tf_op | source)
XLA Modules:
  0.0 285.5 jit_solution(4801848933066637376)
XLA Ops:
  0.0 283.9 %shard_map.82 = bf16[3,192,128]{2,1,0:T(8,128)(2,1)} custom-call(bf16[3,192,128]{2,1,0:T(8,128)(2,1)} %rs.1, bf16[192,3072]{1,0:T(8,128)(2,1)} %il.1, bf16[192,6144]{1,0:T(8,128)(2,1)} %im.1, bf16[192,12288]{1,0:T(8,128)(2,1)} %it.1, bf16[192,3072]{1,0:T(8,128)(2,1)} %ul.1, bf16[192,6144]{1,0:T(8,128)(2,1)} %um.1, s32[16,3072]{1,0:T(8,128)} %sl.1, s32[8,6144]{1,0:T(8,128)} %sm.1), custom_call_target="tpu_custom_call" | custom-call | tf_op jit(solution)/shard_map/pallas_call | solution.py:353
  283.9 1.6 copy.10

commit v3 on v2

--- a/solution.py
+++ b/solution.py
@@ -52,9 +52,6 @@
     def peer(d):
         return (base + flip(d), panel)
 
-    def far_first(k):
-        return jnp.where(k % 2 == 1, 4 + (k + 1) // 2, 4 - k // 2)
-
     def remote(at, src, dst, device):
         return pltpu.make_async_remote_copy(
             src_ref=src, dst_ref=dst, send_sem=send_sem.at[at], recv_sem=recv_sem.at[at],
@@ -83,11 +80,63 @@
         pl.semaphore_signal(barrier, inc=1, device_id=device, device_id_type=MESH)
     pl.semaphore_wait(barrier, len(peers))
 
-    bulk_w1 = [remote(BULK_AT, im.at[:, columns(1 - xi)], w1.at[xi], peer(1))]
-    bulk_v1 = [remote(BULK_AT + 1, um.at[:, columns(1 - xi)], v1.at[xi], peer(1))]
-    bulk_w2 = [
-        remote(BULK_AT + 1 + d, it.at[:, columns(flip(d))], w2.at[x], peer(d)) for d in (1, 2, 3)
-    ]
+    class Bulk:
+        def __init__(self, at, src, cols, dst, device):
+            self.args = at, src, cols, dst, device
+
+        def piece(self, row, rows):
+            at, src, cols, dst, device = self.args
+            return remote(at, src.at[pl.ds(row, rows), cols], dst.at[pl.ds(row, rows)], device)
+
+        def some(self, first, last):
+            for j in range(first, last):
+                self.piece(16 * j, 16).start()
+
+        def start(self):
+            self.some(0, 12)
+
+        def wait_recv(self):
+            self.piece(0, ROWS).wait_recv()
+
+        def wait_send(self):
+            self.piece(0, ROWS).wait_send()
+
+    bulk_v1 = Bulk(BULK_AT, um, columns(1 - xi), v1.at[xi], peer(1))
+    bulk_w1 = Bulk(BULK_AT + 1, im, columns(1 - xi), w1.at[xi], peer(1))
+    bulk_w2 = {d: Bulk(BULK_AT + 1 + d, it, columns(flip(d)), w2.at[x], peer(d)) for d in (1, 2, 3)}
+
+    def when(condition, action):
+        pl.when(condition)(action)
+
+    def start_w2(d):
+        when(x > flip(d), bulk_w2[d].start)
+
+    def arrive_w2():
+        for d in (1, 2, 3):
+            when(x < flip(d), bulk_w2[d].wait_recv)
+
+    def clear_above():
+        @pl.when(xi == 1)
+        def _():
+            w1[0] = jnp.zeros((ROWS, COLS), BF)
+
+        for d in (1, 2, 3):
+            @pl.when(x > flip(d))
+            def _():
+                w2[flip(d)] = jnp.zeros((ROWS, COLS), BF)
+
+    pending = []
+
+    def drain():
+        for action in pending:
+            action()
+        pending.clear()
+
+    def choose(k, table):
+        value = table[-1]
+        for at in range(len(table) - 2, -1, -1):
+            value = jnp.where(k == at, table[at], value)
+        return value
 
     def start(copies):
         for copy in copies:
@@ -96,6 +145,18 @@
     def arrive(copies):
         for copy in copies:
             copy.wait_recv()
+
+    paced = [0]
+
+    def pace():
+        n = paced[0]
+        if n >= 6:
+            return
+        paced[0] += 1
+        for d in (1, 2, 3):
+            @pl.when(x > flip(d))
+            def _():
+                bulk_w2[d].some(2 * n, 2 * n + 2)
 
     counts = {"gather": 0, "reduce": 0, "exchange": 0}
 
@@ -103,41 +164,48 @@
         at = counts["gather"]
         counts["gather"] += 1
         sem = at * PER_PHASE
-        buf = gathers.at[at]
         gathers[at, z, c] = value
 
-        def across(k):
-            own = buf.at[z, c]
-            return remote(sem + k, own, own, chip(far_first(k)))
+        def block(off):
+            return gathers.at[at, ring(off), c]
+
+        def across(k, off, to):
+            return remote(sem + k, block(off), block(off), chip(to))
 
         def source(kk):
-            return ring(-far_first(7 - kk))
+            return choose(kk, (0, 6, 2, 7, 1, 5, 3, 4))
 
         def to_core(kk):
-            block = buf.at[source(kk), c]
-            return remote(sem + 7 + kk, block, block, core)
-
+            own = block(source(kk))
+            return remote(sem + 7 + kk, own, own, core)
+
+        own = [across(k, 0, to) for k, to in ((0, 2), (1, -2), (2, 1), (3, -1), (6, 4))]
+        start(own)
         to_core(0).start()
-
-        def send(k, carry):
-            across(k).start()
-            return carry
-
-        lax.fori_loop(0, 7, send, 0)
+        pace()
+        drain()
         acc[pl.ds(0, nx)] = jnp.zeros((nx, ROWS, VEC), F32)
         if beside is not None:
             beside()
 
         def use(kk):
             to_core(kk).wait_recv()
-            zz = source(kk)
+            zz = ring(source(kk))
             slab = gathers[at, zz].reshape(SLAB, VEC)
             matrix = weight[:, :, lanes(zz)].reshape(nx * ROWS, SLAB)
             got = jnp.dot(matrix, slab, preferred_element_type=F32)
             acc[pl.ds(0, nx)] += got.reshape(nx, ROWS, VEC)
 
+        def forward(kk):
+            return across(3 + kk, source(kk), choose(kk, (0, 1, -1)))
+
         def step(kk, carry):
-            across(7 - kk).wait_recv()
+            across(kk - 1, source(kk), 1).wait_recv()
+
+            @pl.when(kk < 3)
+            def _():
+                forward(kk).start()
+
             to_core(kk).start()
             use(kk - 1)
             return carry
@@ -145,13 +213,16 @@
         lax.fori_loop(1, 8, step, 0)
         use(7)
 
-        def drain(k, carry):
-            across(k).wait_send()
-            to_core(k).wait_send()
-            return carry
-
-        lax.fori_loop(0, 7, drain, 0)
-        to_core(7).wait_send()
+        def finish():
+            def body(k, carry):
+                across(k, 0, 1).wait_send()
+                to_core(k).wait_send()
+                return carry
+
+            lax.fori_loop(0, 7, body, 0)
+            to_core(7).wait_send()
+
+        pending.append(finish)
 
     def apply_reduce(weight, nx):
         at = counts["reduce"]
@@ -159,28 +230,33 @@
         sem = (PHASES + at) * PER_PHASE
 
         def to_core(k):
-            return remote(sem + k, dsend.at[k], core_in.at[at, k], core)
+            return remote(sem + k, dsend.at[at, k], core_in.at[at, k], core)
 
         def across(k):
-            return remote(sem + 8 + k, rsend.at[k], ring_in.at[at, k], chip(far_first(k)))
+            to = choose(k, (1, -1, 4, 1, -1, 2, -2))
+            return remote(sem + 8 + k, rsend.at[at, k], ring_in.at[at, k], chip(to))
 
         def make(k):
-            zz = ring(far_first(k))
+            zz = ring(choose(k, (3, 5, 4, 1, 7, 2, 6, 0)))
             matrix = weight[:, :, lanes(zz)].reshape(nx * ROWS, SLAB)
             right = vals[pl.ds(0, nx)].reshape(nx * ROWS, VEC)
             got = lax.dot_general(
                 matrix, right, (((0,), (0,)), ((), ())), preferred_element_type=F32
             )
             part[k] = got.reshape(CORES, ROWS, VEC)
-            dsend[k] = part[k, 1 - c].astype(BF)
+            dsend[at, k] = part[k, 1 - c].astype(BF)
             to_core(k).start()
 
         def total(k):
             to_core(k).wait_recv()
             return part[k, c] + core_in[at, k].astype(F32)
 
-        def send(k):
-            rsend[k] = total(k).astype(BF)
+        def arrived(k):
+            across(k).wait_recv()
+            return ring_in[at, k].astype(F32)
+
+        def send(k, value):
+            rsend[at, k] = value.astype(BF)
             across(k).start()
 
         def first(k, carry):
@@ -189,45 +265,47 @@
 
         def step(k, carry):
             make(k)
-            send(k - 2)
+            send(k - 2, total(k - 2))
             return carry
 
         lax.fori_loop(0, 2, first, 0)
-        lax.fori_loop(2, 8, step, 0)
-        send(6)
-
-        def collect(i, value):
-            k = 6 - i
-            across(k).wait_recv()
-            return value + ring_in[at, k].astype(F32)
-
-        value = lax.fori_loop(0, 7, collect, total(7))
-
-        def drain(k, carry):
-            across(k).wait_send()
-            to_core(k).wait_send()
-            return carry
-
-        lax.fori_loop(0, 7, drain, 0)
-        to_core(7).wait_send()
+        lax.fori_loop(2, 7, step, 0)
+        make(7)
+        for k in (5, 6):
+            send(k, total(k) + arrived(k - 5))
+        pace()
+        drain()
+        value = total(7)
+        for k in (3, 4, 2, 5, 6):
+            value = value + arrived(k)
+
+        def finish():
+            def body(k, carry):
+                across(k).wait_send()
+                to_core(k).wait_send()
+                return carry
+
+            lax.fori_loop(0, 7, body, 0)
+            to_core(7).wait_send()
+
+        pending.append(finish)
         return value
 
     def exchange(distances, fill, width=1):
         at = counts["exchange"]
         counts["exchange"] += 1
-        copies = {}
+        copies = []
         for d in distances:
-            fill(d)
+            fill(at, d)
             group = pl.ds(d, width)
-            copies[d] = remote(
-                2 * PHASES * PER_PHASE + at * 3 + d - 1, esend.at[group], leaf_in.at[at, group],
-                peer(d),
-            )
-            copies[d].start()
-        for d in distances:
-            copies[d].wait_recv()
-        for d in distances:
-            copies[d].wait_send()
+            copies.append(remote(
+                2 * PHASES * PER_PHASE + at * 3 + d - 1, esend.at[at, group],
+                leaf_in.at[at, group], peer(d),
+            ))
+            copies[-1].start()
+        drain()
+        arrive(copies)
+        pending.extend(copy.wait_send for copy in copies)
         return at
 
     def build_pick(pick, lists, row, first, nx):
@@ -245,39 +323,42 @@
     both = (0, 1)
     every = (1, 2, 3)
 
-    def send_acc(d):
-        esend[d] = acc[flip(d)].astype(BF)
-
-    def send_acc_pair(d):
+    def send_acc(at, d):
+        esend[at, d] = acc[flip(d)].astype(BF)
+
+    def send_acc_pair(at, d):
         for i in both:
-            esend[1 + i] = acc[i].astype(BF)
-
-    start(bulk_w1)
-    mine[0].wait()
-    gather_apply(rs[0], w0, 1, lambda: build_pick(pick0, sl, leaf, 0, 2))
+            esend[at, 1 + i] = acc[i].astype(BF)
+
+    def beside_first():
+        when(xi == 1, bulk_w1.start)
+        build_pick(pick0, sl, leaf, 0, 2)
+        clear_above()
+        mine[0].wait()
+
+    gather_apply(rs[0], w0, 1, beside_first)
     solved[0] = acc[0].astype(BF)
     vals[0] = solved[0]
-    start(bulk_v1)
+    bulk_v1.start()
     mine[1].wait()
     summed = apply_reduce(v0, 1).astype(BF)
     gather_apply(summed, pick0, 2, lambda: build_pick(pick1, sm, leaf // 2, xi, 4))
 
-    def send_other(d):
-        esend[d] = acc[1 - xi].astype(BF)
+    def send_other(at, d):
+        esend[at, d] = acc[1 - xi].astype(BF)
 
     at = exchange((1,), send_other)
     carried = acc[xi] + leaf_in[at, 1].astype(F32)
-    start(bulk_w2)
 
     mine[2].wait()
-    arrive(bulk_w1)
+    when(xi == 0, bulk_w1.wait_recv)
     gather_apply((rs[1].astype(F32) - carried).astype(BF), w1, 2)
     at = exchange((1,), send_acc_pair, 2)
     for i in both:
         solved[1 + i] = (acc[i] + leaf_in[at, 1 + i].astype(F32)).astype(BF)
         vals[i] = solved[1 + i]
     mine[3].wait()
-    arrive(bulk_v1)
+    bulk_v1.wait_recv()
     summed = apply_reduce(v1, 2).astype(BF)
     gather_apply(summed, pick1, 4)
     at = exchange(every, send_acc)
@@ -286,7 +367,7 @@
         carried = carried + leaf_in[at, d].astype(F32)
 
     mine[4].wait()
-    arrive(bulk_w2)
+    arrive_w2()
     gather_apply((rs[2].astype(F32) - carried).astype(BF), w2, 4)
     at = exchange(every, send_acc)
     top = acc[x]
@@ -294,8 +375,8 @@
         top = top + leaf_in[at, d].astype(F32)
 
     def share(value, distances):
-        def fill(d):
-            esend[d] = value
+        def fill(at, d):
+            esend[at, d] = value
 
         at = exchange(distances, fill)
         if len(distances) == 1:
@@ -326,8 +407,11 @@
     vals[0] = (solved[0].astype(F32) - acc[0]).astype(BF)
     out[0] = apply_reduce(w0, 1).astype(BF)
 
-    for copy in bulk_w1 + bulk_v1 + bulk_w2:
-        copy.wait_send()
+    drain()
+    bulk_v1.wait_send()
+    when(xi == 1, bulk_w1.wait_send)
+    for d in every:
+        when(x > flip(d), bulk_w2[d].wait_send)
 
 
 def on_device(*args):
@@ -341,9 +425,9 @@
         pltpu.VMEM((PHASES, RING, ROWS, VEC), BF),
         pltpu.VMEM((PHASES, RING, ROWS, VEC), BF),
         pltpu.VMEM((EXCHANGES, 4, ROWS, VEC), BF),
-        pltpu.VMEM((RING, ROWS, VEC), BF),
-        pltpu.VMEM((RING, ROWS, VEC), BF),
-        pltpu.VMEM((4, ROWS, VEC), BF),
+        pltpu.VMEM((PHASES, RING, ROWS, VEC), BF),
+        pltpu.VMEM((PHASES, RING, ROWS, VEC), BF),
+        pltpu.VMEM((EXCHANGES, 4, ROWS, VEC), BF),
         pltpu.VMEM((4, ROWS, VEC), BF),
         pltpu.VMEM((3, ROWS, VEC), BF),
         pltpu.SemaphoreType.DMA((5,)),

time: 287 us -> 249 us (0.87)
  Pallas kernels: 284 us -> 247 us
    pallas_call x1, Pallas kernels: 284 us -> 247 us  [on_device(): pl.pallas_call(kernel, out_shape=jax.ShapeDtypeStruct((3, ROWS, VEC), BF)...]
where the time goes in v3:
time: 249 us
  Pallas kernels  247 us (99%)
    pallas_call x1, Pallas kernels, on_device(): pl.pallas_call(kernel, out_shape=jax.ShapeDtypeStruct((3, ROWS, VEC), BF)...  247 us

profile of v3, /device:TPU:7, one launch (start us, length us, event | category | flops | bytes accessed | tf_op | source)
XLA Modules:
  0.0 249.0 jit_solution(16688840588692153195)
XLA Ops:
  0.0 247.4 %shard_map.82 = bf16[3,192,128]{2,1,0:T(8,128)(2,1)} custom-call(bf16[3,192,128]{2,1,0:T(8,128)(2,1)} %rs.1, bf16[192,3072]{1,0:T(8,128)(2,1)} %il.1, bf16[192,6144]{1,0:T(8,128)(2,1)} %im.1, bf16[192,12288]{1,0:T(8,128)(2,1)} %it.1, bf16[192,3072]{1,0:T(8,128)(2,1)} %ul.1, bf16[192,6144]{1,0:T(8,128)(2,1)} %um.1, s32[16,3072]{1,0:T(8,128)} %sl.1, s32[8,6144]{1,0:T(8,128)} %sm.1), custom_call_target="tpu_custom_call" | custom-call | tf_op jit(solution)/shard_map/pallas_call | solution.py:437
  247.4 1.6 copy.10

commit v4 on v3

--- a/solution.py
+++ b/solution.py
@@ -35,7 +35,7 @@
     base = leaf - x
 
     def ring(off):
-        return (z + off + RING) % RING
+        return (z + off) & (RING - 1)
 
     def chip(off):
         return (leaf, ring(off) * 2 + c)
@@ -108,9 +108,6 @@
     def when(condition, action):
         pl.when(condition)(action)
 
-    def start_w2(d):
-        when(x > flip(d), bulk_w2[d].start)
-
     def arrive_w2():
         for d in (1, 2, 3):
             when(x < flip(d), bulk_w2[d].wait_recv)
@@ -133,10 +130,8 @@
         pending.clear()
 
     def choose(k, table):
-        value = table[-1]
-        for at in range(len(table) - 2, -1, -1):
-            value = jnp.where(k == at, table[at], value)
-        return value
+        packed = sum((entry % RING) << (3 * at) for at, entry in enumerate(table))
+        return (packed >> (3 * k)) & (RING - 1)
 
     def start(copies):
         for copy in copies:
@@ -146,17 +141,24 @@
         for copy in copies:
             copy.wait_recv()
 
-    paced = [0]
-
-    def pace():
-        n = paced[0]
-        if n >= 6:
-            return
-        paced[0] += 1
-        for d in (1, 2, 3):
-            @pl.when(x > flip(d))
-            def _():
-                bulk_w2[d].some(2 * n, 2 * n + 2)
+    bulk_of = {"w1": [(bulk_w1, xi == 1)], "v1": [(bulk_v1, None)]}
+    bulk_of["w2"] = [(bulk_w2[d], x > flip(d)) for d in (1, 2, 3)]
+    plan = {'g0': [('w1', 6)], 'r0': [('w1', 6), ('v1', 2)], 'g1': [('v1', 4), ('w2', 1)], 'e0': [('v1', 3), ('w2', 2)], 'g2': [('v1', 3), ('w2', 2)], 'e1': [('w2', 3)], 'r1': [('w2', 2)], 'g3': [('w2', 1)], 'e2': [('w2', 1)]}
+    sent = {"w1": 0, "v1": 0, "w2": 0}
+
+    def pace(slot, also=None):
+        for key, number in plan.get(slot, ()):
+            first = sent[key]
+            sent[key] += number
+            for bulk, condition in bulk_of[key]:
+                if condition is None or also is None:
+                    ready = also if condition is None else condition
+                else:
+                    ready = jnp.logical_and(also, condition)
+                if ready is None:
+                    bulk.some(first, first + number)
+                else:
+                    when(ready, lambda bulk=bulk: bulk.some(first, first + number))
 
     counts = {"gather": 0, "reduce": 0, "exchange": 0}
 
@@ -182,7 +184,6 @@
         own = [across(k, 0, to) for k, to in ((0, 2), (1, -2), (2, 1), (3, -1), (6, 4))]
         start(own)
         to_core(0).start()
-        pace()
         drain()
         acc[pl.ds(0, nx)] = jnp.zeros((nx, ROWS, VEC), F32)
         if beside is not None:
@@ -205,6 +206,8 @@
             @pl.when(kk < 3)
             def _():
                 forward(kk).start()
+
+            pace(f"g{at}", kk == 3)
 
             to_core(kk).start()
             use(kk - 1)
@@ -273,7 +276,7 @@
         make(7)
         for k in (5, 6):
             send(k, total(k) + arrived(k - 5))
-        pace()
+        pace(f"r{at}")
         drain()
         value = total(7)
         for k in (3, 4, 2, 5, 6):
@@ -303,6 +306,7 @@
                 leaf_in.at[at, group], peer(d),
             ))
             copies[-1].start()
+        pace(f"e{at}")
         drain()
         arrive(copies)
         pending.extend(copy.wait_send for copy in copies)
@@ -331,7 +335,6 @@
             esend[at, 1 + i] = acc[i].astype(BF)
 
     def beside_first():
-        when(xi == 1, bulk_w1.start)
         build_pick(pick0, sl, leaf, 0, 2)
         clear_above()
         mine[0].wait()
@@ -339,7 +342,6 @@
     gather_apply(rs[0], w0, 1, beside_first)
     solved[0] = acc[0].astype(BF)
     vals[0] = solved[0]
-    bulk_v1.start()
     mine[1].wait()
     summed = apply_reduce(v0, 1).astype(BF)
     gather_apply(summed, pick0, 2, lambda: build_pick(pick1, sm, leaf // 2, xi, 4))

time: 249 us -> 244 us (0.980); the launches traced: 249 us -> 239 us
  Pallas kernels: 247 us -> 237 us
    pallas_call x1, Pallas kernels: 247 us -> 237 us  [on_device(): pl.pallas_call(kernel, out_shape=jax.ShapeDtypeStruct((3, ROWS, VEC), BF)...]
where the time goes in v4:
time: 244 us; the launch traced here: 239 us
  Pallas kernels  237 us (97%)
    pallas_call x1, Pallas kernels, on_device(): pl.pallas_call(kernel, out_shape=jax.ShapeDtypeStruct((3, ROWS, VEC), BF)...  237 us

profile of v4, /device:TPU:7, one launch (start us, length us, event | category | flops | bytes accessed | tf_op | source)
XLA Modules:
  0.0 239.0 jit_solution(4758722934260009579)
XLA Ops:
  0.0 237.4 %shard_map.82 = bf16[3,192,128]{2,1,0:T(8,128)(2,1)} custom-call(bf16[3,192,128]{2,1,0:T(8,128)(2,1)} %rs.1, bf16[192,3072]{1,0:T(8,128)(2,1)} %il.1, bf16[192,6144]{1,0:T(8,128)(2,1)} %im.1, bf16[192,12288]{1,0:T(8,128)(2,1)} %it.1, bf16[192,3072]{1,0:T(8,128)(2,1)} %ul.1, bf16[192,6144]{1,0:T(8,128)(2,1)} %um.1, s32[16,3072]{1,0:T(8,128)} %sl.1, s32[8,6144]{1,0:T(8,128)} %sm.1), custom_call_target="tpu_custom_call" | custom-call | tf_op jit(solution)/shard_map/pallas_call | solution.py:439
  237.4 1.6 copy.10

commit v5 on v4

--- a/solution.py
+++ b/solution.py
@@ -207,7 +207,7 @@
             def _():
                 forward(kk).start()
 
-            pace(f"g{at}", kk == 3)
+            pace(f"g{at}", kk == 2)
 
             to_core(kk).start()
             use(kk - 1)
@@ -268,12 +268,13 @@
 
         def step(k, carry):
             make(k)
-            send(k - 2, total(k - 2))
+            send(k - lag, total(k - lag))
             return carry
 
-        lax.fori_loop(0, 2, first, 0)
-        lax.fori_loop(2, 7, step, 0)
-        make(7)
+        lag = 1 if nx == 4 else 2
+        lax.fori_loop(0, lag, first, 0)
+        lax.fori_loop(lag, 5 + lag, step, 0)
+        lax.fori_loop(5 + lag, 8, first, 0)
         for k in (5, 6):
             send(k, total(k) + arrived(k - 5))
         pace(f"r{at}")

time: 244 us -> 240 us (0.984); the launches traced: 239 us -> 240 us
  no operation moved by 1% of the time
where the time goes in v5:
time: 240 us
  Pallas kernels  238 us (99%)
    pallas_call x1, Pallas kernels, on_device(): pl.pallas_call(kernel, out_shape=jax.ShapeDtypeStruct((3, ROWS, VEC), BF)...  238 us

profile of v5, /device:TPU:7, one launch (start us, length us, event | category | flops | bytes accessed | tf_op | source)
XLA Modules:
  0.0 239.9 jit_solution(18443459907329176723)
XLA Ops:
  0.0 238.3 %shard_map.82 = bf16[3,192,128]{2,1,0:T(8,128)(2,1)} custom-call(bf16[3,192,128]{2,1,0:T(8,128)(2,1)} %rs.1, bf16[192,3072]{1,0:T(8,128)(2,1)} %il.1, bf16[192,6144]{1,0:T(8,128)(2,1)} %im.1, bf16[192,12288]{1,0:T(8,128)(2,1)} %it.1, bf16[192,3072]{1,0:T(8,128)(2,1)} %ul.1, bf16[192,6144]{1,0:T(8,128)(2,1)} %um.1, s32[16,3072]{1,0:T(8,128)} %sl.1, s32[8,6144]{1,0:T(8,128)} %sm.1), custom_call_target="tpu_custom_call" | custom-call | tf_op jit(solution)/shard_map/pallas_call | solution.py:440
  238.3 1.6 copy.10
